TPU v7x, 256 devices: a whole 4x4x8 slice. The times are simulated.
256 devices in a mesh: seq: 128 (over y_lo, x, z, core), req: 2 (over y_hi).
Axes of the slice: x: 4, y: 4 (y_hi: 2, y_lo: 2; y = y_hi * 2 + y_lo), z: 8, core: 2. Of those that a mesh axis runs over, the one named last changes fastest.
Arguments:
- tokens: bfloat16 [16384, 2048], P('seq'), may hold values from -6 to 6
- norm_gain: float32 [2048], replicated, may hold values from 0.5 to 1.5
- w_query: bfloat16 [2048, 1024], P(None, 'req'), as said below
- key_projection: bfloat16 [2048, 512], P(None, 'req')
- value_projection: bfloat16 [2048, 512], P(None, 'req'), may hold values from -0.125 to 0.125
- w_out: bfloat16 [1024, 2048], P('req'), may hold values from -0.1875 to 0.1875
- lengths: int32 [4], replicated, may hold values from 1 to 10922, 16384 in all
- block_split: int32 [128], replicated, may hold values from 0 to 127, each once
- page_slot: int32 [512], replicated, may hold values from 0 to 1023, as said below
Outputs:
- hidden: bfloat16 [16384, 2048], P(('seq', 'req'))
- key_value_cache: bfloat16 [1024, 2, 32, 512], P('seq', None, None, 'req')
Inputs may be any that keep to these rules, and one draw needn't show every extreme that they name: block_split is a permutation; index i of seq holds block block_split[i] and its mirror. `page_slot`: distinct slots; slot s lies on index s // 8 of seq. `w_query`: a projection scaled like 2 / sqrt(2048).
All inputs are finite; a program needn't handle non-finite values.
Results may differ from a plain program's by a relative error of at most 0.014.
The roundings to bfloat16 on the way count: a program that leaves them out, or rounds other values in their place, can miss the bound.
Values may be sent and summed in bfloat16 or wider, within the bound.
A program may use at most 128 MiB of HBM per device.

v0:
```python
import math
import jax
import jax.numpy as jnp
from jax import lax
from jax.sharding import PartitionSpec as P

HEAD_SIZE = 128
PAGE_TOKENS = 32
theta_base = 1000000.0
norm_eps = 1e-05
far_below = -1e30


def rotary_rows(heads, offset_list):
    half_width = heads.shape[-1] // 2
    exponent = jnp.arange(half_width, dtype=jnp.float32) * (2.0 / heads.shape[-1])
    inv_freq = jnp.power(theta_base, -exponent)
    angle = offset_list.astype(jnp.float32)[:, None] * inv_freq[None, :]
    cosine = jnp.concatenate([jnp.cos(angle), jnp.cos(angle)], -1)[:, None, :]
    sine = jnp.concatenate([jnp.sin(angle), jnp.sin(angle)], -1)[:, None, :]
    rolled = jnp.concatenate([-heads[..., half_width:], heads[..., :half_width]], -1)
    return heads * cosine + rolled * sine


def slot_positions(block_split, lengths, total_rows, shard_rows):
    row_ids = jnp.arange(total_rows, dtype=jnp.int32)
    half_rows = shard_rows // 2
    cycle_size = block_split.shape[0]
    owner_dev = row_ids // shard_rows
    device_ids = jnp.arange(cycle_size, dtype=jnp.int32)
    first_block = jnp.sum(
        jnp.where(owner_dev[:, None] == device_ids[None, :], block_split[None, :], 0), 1
    )
    block_ids = jnp.where(
        row_ids % shard_rows < half_rows, first_block, 2 * cycle_size - 1 - first_block
    )
    position = block_ids * half_rows + row_ids % half_rows
    request_ends = jnp.cumsum(lengths)
    request_begins = request_ends - lengths
    request = jnp.sum((position[:, None] >= request_ends[None, :]).astype(jnp.int32), 1)
    prompt_ids = jnp.arange(lengths.shape[0], dtype=jnp.int32)
    begins = jnp.sum(
        jnp.where(request[:, None] == prompt_ids[None, :], request_begins[None, :], 0), 1
    )
    return (position, request, position - begins)


def on_device(
    tokens,
    norm_gain,
    w_query,
    key_projection,
    value_projection,
    w_out,
    lengths,
    block_split,
    page_slot,
):
    shard_rows = tokens.shape[0]
    half_rows = shard_rows // 2
    cycle_size = lax.axis_size("seq")
    device = lax.axis_index("seq")
    first_row = device * shard_rows
    position, request, offset_list = slot_positions(
        block_split, lengths, shard_rows * cycle_size, shard_rows
    )
    q_pos = lax.dynamic_slice_in_dim(position, first_row, shard_rows, 0)
    q_req = lax.dynamic_slice_in_dim(request, first_row, shard_rows, 0)
    q_off = lax.dynamic_slice_in_dim(offset_list, first_row, shard_rows, 0)
    cache_rows = 2 * shard_rows
    slot_count = cache_rows // PAGE_TOKENS
    slot_ids = page_slot[position // PAGE_TOKENS]
    holder = slot_ids // slot_count
    target_rows = jnp.where(
        holder == device, slot_ids % slot_count * PAGE_TOKENS + position % PAGE_TOKENS, -1
    )
    heads_local = w_query.shape[1] // HEAD_SIZE
    kv_local = key_projection.shape[1] // HEAD_SIZE
    group_width = heads_local // kv_local
    scale_factor = 1.0 / math.sqrt(HEAD_SIZE)
    widened = tokens.astype(jnp.float32)
    normalized_input = (
        widened * lax.rsqrt(jnp.mean(widened * widened, -1, keepdims=True) + norm_eps) * norm_gain
    ).astype(jnp.bfloat16)
    queries = rotary_rows(
        jnp.dot(normalized_input, w_query, preferred_element_type=jnp.float32).reshape(
            shard_rows, heads_local, HEAD_SIZE
        ),
        q_off,
    )
    queries = queries.astype(jnp.bfloat16).reshape(shard_rows, kv_local, group_width, HEAD_SIZE)
    key_matrix_rows = rotary_rows(
        jnp.dot(normalized_input, key_projection, preferred_element_type=jnp.float32).reshape(
            shard_rows, kv_local, HEAD_SIZE
        ),
        q_off,
    )
    key_matrix_rows = key_matrix_rows.astype(jnp.bfloat16).reshape(shard_rows, kv_local * HEAD_SIZE)
    value_matrix_rows = jnp.dot(
        normalized_input, value_projection, preferred_element_type=jnp.float32
    ).astype(jnp.bfloat16)

    def attend(moments, key_block, value_block, visible):
        run_max, run_sum, run_acc = moments
        width = key_block.shape[0]
        key_heads = key_block.reshape(width, kv_local, HEAD_SIZE)
        value_heads = value_block.reshape(width, kv_local, HEAD_SIZE)
        scores = (
            jnp.einsum("qhgd,khd->hgqk", queries, key_heads, preferred_element_type=jnp.float32)
            * scale_factor
        )
        masked = jnp.where(visible[None, None], scores, far_below)
        new_max = jnp.maximum(run_max, jnp.max(masked, -1))
        weights = jnp.where(visible[None, None], jnp.exp(masked - new_max[..., None]), 0.0)
        factor = jnp.exp(run_max - new_max)
        new_sum = run_sum * factor + jnp.sum(weights, -1)
        added = jnp.einsum(
            "hgqk,khd->hgqd",
            weights.astype(jnp.bfloat16),
            value_heads,
            preferred_element_type=jnp.float32,
        )
        return (new_max, new_sum, run_acc * factor[..., None] + added)

    def store(parts, key_block, value_block, key_target):
        cache_grid = jnp.arange(cache_rows, dtype=jnp.int32)
        placer = (cache_grid[:, None] == key_target[None, :]).astype(jnp.bfloat16)
        return (
            parts[0] + jnp.dot(placer, key_block, preferred_element_type=jnp.float32),
            parts[1] + jnp.dot(placer, value_block, preferred_element_type=jnp.float32),
        )

    start_max = jnp.full((kv_local, group_width, shard_rows), far_below, jnp.float32)
    start_sum = jnp.zeros((kv_local, group_width, shard_rows), jnp.float32)
    start_acc = jnp.zeros((kv_local, group_width, shard_rows, HEAD_SIZE), jnp.float32)
    start_keys = jnp.zeros((cache_rows, kv_local * HEAD_SIZE), jnp.float32)
    start_values = jnp.zeros((cache_rows, kv_local * HEAD_SIZE), jnp.float32)
    state = (start_max, start_sum, start_acc, start_keys, start_values)
    absorb_state = state
    key_piece = lax.all_gather(key_matrix_rows, "seq", axis=0, tiled=True)
    value_piece = lax.all_gather(value_matrix_rows, "seq", axis=0, tiled=True)
    length = key_piece.shape[0]
    sub_width = math.gcd(length, 1024)

    def sub_step(carried, sub_index):
        offset = sub_index * sub_width
        key_block = lax.dynamic_slice_in_dim(key_piece, offset, sub_width, 0)
        value_block = lax.dynamic_slice_in_dim(value_piece, offset, sub_width, 0)
        key_pos = lax.dynamic_slice_in_dim(position, offset, sub_width, 0)
        key_req = lax.dynamic_slice_in_dim(request, offset, sub_width, 0)
        key_target = lax.dynamic_slice_in_dim(target_rows, offset, sub_width, 0)
        visible = (key_req[None, :] == q_req[:, None]) & (key_pos[None, :] <= q_pos[:, None])
        moments = carried[:3]
        cache_parts = carried[3:]
        moments = attend(moments, key_block, value_block, visible)
        cache_parts = lax.cond(
            jnp.any(key_target >= 0),
            store,
            lambda parts, key_block, value_block, key_target: parts,
            cache_parts,
            key_block,
            value_block,
            key_target,
        )
        return (moments + cache_parts, None)

    absorb_state, _ = lax.scan(
        sub_step, absorb_state, jnp.arange(length // sub_width, dtype=jnp.int32)
    )
    state = absorb_state
    run_max, run_sum, run_acc, cache_keys, cache_values = state
    normalised = run_acc / run_sum[..., None]
    context = (
        jnp.transpose(normalised, (2, 0, 1, 3))
        .reshape(shard_rows, heads_local * HEAD_SIZE)
        .astype(jnp.bfloat16)
    )
    summed = lax.psum_scatter(
        jnp.dot(context, w_out, preferred_element_type=jnp.float32).astype(jnp.bfloat16),
        "req",
        scatter_dimension=0,
        tiled=True,
    ).astype(jnp.float32)
    residual = lax.dynamic_slice_in_dim(tokens, lax.axis_index("req") * half_rows, half_rows, 0)
    hidden = (summed + residual.astype(jnp.float32)).astype(jnp.bfloat16)
    key_value_cache = jnp.stack(
        [
            cache_keys.reshape(slot_count, PAGE_TOKENS, kv_local * HEAD_SIZE),
            cache_values.reshape(slot_count, PAGE_TOKENS, kv_local * HEAD_SIZE),
        ],
        1,
    ).astype(jnp.bfloat16)
    return (hidden, key_value_cache)


def solution(mesh):
    in_specs = (
        P("seq", None),
        P(),
        P(None, "req"),
        P(None, "req"),
        P(None, "req"),
        P("req", None),
        P(),
        P(),
        P(),
    )
    out_specs = (P(("seq", "req"), None), P("seq", None, None, "req"))
    return jax.shard_map(
        on_device, mesh=mesh, in_specs=in_specs, out_specs=out_specs, check_vma=False
    )
```

profile of v0, /device:TPU:1, one launch (start us, length us, event | category | flops | bytes accessed | tf_op | source)
XLA Modules:
  0.0 716.6 jit_solution(10461966883109596945)
XLA Ops:
  8.7 2.4 convolution_convert_fusion.1
  11.3 1.6 fusion.44
  13.0 5.1 select_reduce_fusion
  18.6 101.9 %gather_fusion = s32[16384]{0:T(1024)S(1)} fusion(s32[512]{0:T(512)S(1)} %copy-done.1, s32[16384]{0:T(1024)S(1)} %broadcast_clamp_fusion), kind=kCustom, calls=%fused_computation | custom fusion | bytes 196608 | tf_op jit(solution)/shard_map/gather | solution.py:72
  124.2 2.1 fusion.42
  127.7 107.3 %all-gather.5.cloned.1.call-done = bf16[16384,256]{1,0:T(8,128)(2,1)} async-done(((bf16[128,256]{1,0:T(8,128)(2,1)}), bf16[16384,256]{1,0:T(8,128)(2,1)}) %all-gather.5.cloned.1.call-update) | async-done | bytes 8388624 | tf_op jit(solution)/shard_map/all_gather | solution.py:141
  235.0 222.0 %all-gather.3.cloned.1.call-done = bf16[16384,256]{1,0:T(8,128)(2,1)} async-done(((bf16[128,256]{1,0:T(8,128)(2,1)}), bf16[16384,256]{1,0:T(8,128)(2,1)}) %all-gather.3.cloned.1.call-update) | async-done | bytes 8388624 | tf_op jit(solution)/shard_map/all_gather | solution.py:140
  458.4 229.8 %while.19 = (s32[]{:T(128)}, f32[2,2,128]{2,1,0:T(2,128)S(1)}, f32[2,2,128]{2,1,0:T(2,128)S(1)}, f32[2,2,128,128]{3,2,1,0:T(8,128)}, f32[256,256]{1,0:T(8,128)},...) while((s32[]{:T(128)}, f32[2,2,128]{2,1,0:T(2,128)S(1)}, ...), condition=%wide.region_11.12_spmd.clone, body=%wide.region_5.11_spmd.clone.sunk | while | flops 544936448 | bytes 20653632 | solution.py:167
  460.4 1.4 compare_reduce_fusion.2
  463.4 2.1 constant_dynamic-slice_fusion.3
  473.4 1.4 compare_reduce_fusion.2
  476.5 2.1 constant_dynamic-slice_fusion.3
  486.5 1.4 compare_reduce_fusion.2
  489.6 2.1 constant_dynamic-slice_fusion.3
  499.6 1.4 compare_reduce_fusion.2
  502.6 2.1 constant_dynamic-slice_fusion.3
  512.7 1.4 compare_reduce_fusion.2
  515.7 2.1 constant_dynamic-slice_fusion.3
  520.1 3.5 conditional.3
  520.1 1.5 convolution_add_fusion
  521.5 2.0 convolution_add_fusion.1
  528.3 1.4 compare_reduce_fusion.2
  531.4 2.1 constant_dynamic-slice_fusion.3
  535.7 3.5 conditional.3
  535.7 1.5 convolution_add_fusion
  537.2 2.0 convolution_add_fusion.1
  547.0 2.1 constant_dynamic-slice_fusion.3
  557.0 1.4 compare_reduce_fusion.2
  560.1 2.1 constant_dynamic-slice_fusion.3
  564.5 3.5 conditional.3
  564.5 1.5 convolution_add_fusion
  565.9 2.0 convolution_add_fusion.1
  572.7 1.4 compare_reduce_fusion.2
  575.8 2.1 constant_dynamic-slice_fusion.3
  580.1 3.5 conditional.3
  580.1 1.5 convolution_add_fusion
  581.6 2.0 convolution_add_fusion.1
  588.4 1.4 compare_reduce_fusion.2
  591.4 2.1 constant_dynamic-slice_fusion.3
  595.8 3.5 conditional.3
  595.8 1.5 convolution_add_fusion
  597.3 2.0 convolution_add_fusion.1
  604.0 1.4 compare_reduce_fusion.2
  607.1 2.1 constant_dynamic-slice_fusion.3
  611.4 3.5 conditional.3
  611.4 1.5 convolution_add_fusion
  612.9 2.0 convolution_add_fusion.1
  619.7 1.4 compare_reduce_fusion.2
  622.7 2.1 constant_dynamic-slice_fusion.3
  632.8 1.4 compare_reduce_fusion.2
  635.8 2.1 constant_dynamic-slice_fusion.3
  645.8 1.4 compare_reduce_fusion.2
  648.9 2.1 constant_dynamic-slice_fusion.3
  658.9 1.4 compare_reduce_fusion.2
  662.0 2.1 constant_dynamic-slice_fusion.3
  666.3 3.5 conditional.3
  666.3 1.5 convolution_add_fusion
  667.8 2.0 convolution_add_fusion.1
  677.6 2.1 constant_dynamic-slice_fusion.3
  682.0 3.5 conditional.3
  682.0 1.5 convolution_add_fusion
  683.5 2.0 convolution_add_fusion.1
  691.5 16.9 %reduce-scatter.2.cloned.1.call-done = bf16[64,2048]{1,0:T(8,128)(2,1)} async-done(((bf16[128,2048]{1,0:T(8,128)(2,1)}), bf16[64,2048]{1,0:T(8,128)(2,1)}) %reduce-scatter.2.cloned.1.call-update) | async-done | bytes 262160 | tf_op jit(solution)/shard_map/reduce_scatter | solution.py:178
  708.4 1.7 add_convert_fusion
  (518 shorter events, 138.6 us)
Async XLA Ops:
  7.2 682.2 %copy-start = (bf16[512,2048]{1,0:T(8,128)(2,1)S(1)}, bf16[512,2048]{1,0:T(8,128)(2,1)}, u32[]{:S(2)}) copy-start(bf16[512,2048]{1,0:T(8,128)(2,1)} %param.18) | copy-start | bytes 6291460
  7.2 4.1 copy-start.5
  7.2 4.1 copy-start.13
  7.2 3.9 copy-start.15
  7.2 227.8 %all-gather.5.cloned.1.call-start = ((), (), s32[]{:S(2)}) async-start(), calls=%async_computation.2 | async-start | bytes 8454144 | tf_op jit(solution)/shard_map/all_gather | solution.py:141
  8.6 4.4 copy-start.14
  8.7 10.0 %copy-start.1 = (s32[512]{0:T(512)S(1)}, s32[512]{0:T(512)}, u32[]{:S(2)}) copy-start(s32[512]{0:T(512)} %param.21) | copy-start | bytes 6148
  11.1 446.0 %all-gather.3.cloned.1.call-start = ((), (), s32[]{:S(2)}) async-start(), calls=%async_computation.1 | async-start | bytes 8454144 | tf_op jit(solution)/shard_map/all_gather | solution.py:140
  123.5 584.9 %reduce-scatter.2.cloned.1.call-start = ((), (), s32[]{:S(2)}) async-start(), calls=%async_computation.3 | async-start | bytes 786432 | tf_op jit(solution)/shard_map/reduce_scatter | solution.py:178
  458.4 4.0 copy-start.7
  458.4 4.0 copy-start.9
  471.4 4.0 copy-start.7
  471.4 4.0 copy-start.9
  482.9 1.6 copy-start.8
  484.5 4.0 copy-start.7
  484.5 4.0 copy-start.9
  495.9 1.6 copy-start.8
  497.6 4.0 copy-start.7
  497.6 4.0 copy-start.9
  509.0 1.6 copy-start.8
  510.6 4.0 copy-start.7
  510.7 4.0 copy-start.9
  520.1 3.5 copy-start.4
  524.7 1.6 copy-start.8
  526.3 4.0 copy-start.7
  526.3 4.0 copy-start.9
  535.7 3.5 copy-start.4
  540.3 1.6 copy-start.8
  542.0 4.0 copy-start.7
  542.0 4.0 copy-start.9
  553.4 1.6 copy-start.8
  555.0 4.0 copy-start.7
  555.0 4.0 copy-start.9
  564.5 3.5 copy-start.4
  569.1 1.6 copy-start.8
  570.7 4.0 copy-start.7
  570.7 4.0 copy-start.9
  580.1 3.5 copy-start.4
  584.7 1.6 copy-start.8
  586.4 4.0 copy-start.7
  586.4 4.0 copy-start.9
  595.8 3.5 copy-start.4
  600.4 1.6 copy-start.8
  602.0 4.0 copy-start.7
  602.0 4.0 copy-start.9
  611.4 3.5 copy-start.4
  616.0 1.6 copy-start.8
  617.7 4.0 copy-start.7
  617.7 4.0 copy-start.9
  629.1 1.6 copy-start.8
  630.7 4.0 copy-start.7
  630.8 4.0 copy-start.9
  642.2 1.6 copy-start.8
  643.8 4.0 copy-start.7
  643.8 4.0 copy-start.9
  656.9 4.0 copy-start.7
  656.9 4.0 copy-start.9
  666.3 3.5 copy-start.4
  670.9 1.6 copy-start.8
  672.6 4.0 copy-start.7
  672.6 4.0 copy-start.9
  682.0 3.5 copy-start.4
  688.2 2.5 copy-start.3
  689.4 19.0 %copy-start.6 = (bf16[128,2048]{1,0:T(8,128)(2,1)S(1)}, bf16[128,2048]{1,0:T(8,128)(2,1)}, u32[]{:S(2)}) copy-start(bf16[128,2048]{1,0:T(8,128)(2,1)} %param.13) | copy-start | bytes 1572868
  (75 other events, 84.5 us)
Sparse Core Ops, SparseCore 0:
  11.2 223.7 all-gather.4
  237.5 219.5 all-gather.2
  690.8 17.5 reduce-scatter.1
where the time goes:
time: 720 us; the launch traced here: 717 us
  waiting for transfers between devices  346 us (48%)
  local copies, waits for them, and re-layouts  216 us (30%)
  other arithmetic  60.5 us (8%)
  matrix products  57.7 us (8%)
  loops' own time  22.4 us (3%)
  between operations  14.1 us (2%)
    all_gather x1, waiting for transfers between devices, on_device(): key_piece = lax.all_gather(key_matrix_rows, 'seq', axis=0, tiled=True)  222 us
    all_gather x1, waiting for transfers between devices, on_device(): value_piece = lax.all_gather(value_matrix_rows, 'seq', axis=0, tiled=True)  107 us
    gather x1, local copies, waits for them, and re-layouts, on_device(): slot_ids = page_slot[position // PAGE_TOKENS]  102 us
    dynamic_slice x32, local copies, waits for them, and re-layouts, sub_step(): value_block = lax.dynamic_slice_in_dim(value_piece, offset, sub_width, 0)  49.8 us
    another operation x1, loops' own time, on_device(): lax.scan(sub_step, absorb_state, jnp.arange(length // sub_width, dtype=jn...  22.3 us
    reduce_or x16, other arithmetic, sub_step(): jnp.any(key_target >= 0)  22.2 us
    dynamic_slice x16, local copies, waits for them, and re-layouts, on_device(): lax.scan(sub_step, absorb_state, jnp.arange(length // sub_width, dtype=jn...  21 us
    dynamic_slice x16, local copies, waits for them, and re-layouts, sub_step(): key_block = lax.dynamic_slice_in_dim(key_piece, offset, sub_width, 0)  19.9 us
  transfers between devices with their start and end apart: 3, of which 3 were waited for; matrix products, arithmetic and copies ran while one was open for 16% of the time, Pallas kernels for 0%

commit v1 on v0

--- a/solution.py
+++ b/solution.py
@@ -138,7 +138,10 @@
     state = (start_max, start_sum, start_acc, start_keys, start_values)
     absorb_state = state
     key_piece = lax.all_gather(key_matrix_rows, "seq", axis=0, tiled=True)
-    value_piece = lax.all_gather(value_matrix_rows, "seq", axis=0, tiled=True)
+    size = lax.axis_size("seq")
+    tiles = jnp.stack([value_matrix_rows for _ in range(size)])
+    tiles = lax.all_to_all(tiles, "seq", split_axis=0, concat_axis=0)
+    value_piece = jnp.concatenate(tiles, axis=0)
     length = key_piece.shape[0]
     sub_width = math.gcd(length, 1024)
 

time: 720 us -> 754 us (1.047)
  waiting for transfers between devices: 346 us -> 240 us
  matrix products: 57.7 us -> 123 us
  other arithmetic: 60.5 us -> 97.6 us
  local copies, waits for them, and re-layouts: 216 us -> 235 us
  starting transfers between devices: 0.12 us -> 15.6 us
    all_gather x1 -> x0, waiting for transfers between devices: 107 us -> none  [on_device(): value_piece = lax.all_gather(value_matrix_rows, 'seq', axis=0, tiled=True)]
    all_gather x1, waiting for transfers between devices: 222 us -> 149 us  [on_device(): key_piece = lax.all_gather(key_matrix_rows, 'seq', axis=0, tiled=True)]
    all_to_all x0 -> x1, waiting for transfers between devices: none -> 69.1 us  [on_device(): tiles = lax.all_to_all(tiles, 'seq', split_axis=0, concat_axis=0)]
    dot_general x16, matrix products: 14.4 us -> 53.3 us  [attend(): jnp.einsum('hgqk,khd->hgqd', weights.astype(jnp.bfloat16), value_heads, p...]
    dot_general x16, matrix products: 8.18 us -> 43.9 us  [attend(): jnp.einsum('qhgd,khd->hgqk', queries, key_heads, preferred_element_type=j...]
    reduce_sum x16, other arithmetic: 8.53 us -> 33.9 us  [attend(): new_sum = run_sum * factor + jnp.sum(weights, -1)]
    while x272 -> x48, local copies, waits for them, and re-layouts: 18.8 us -> 0.08 us
    all_to_all x0 -> x1, starting transfers between devices: none -> 15.4 us  [on_device(): tiles = lax.all_to_all(tiles, 'seq', split_axis=0, concat_axis=0)]
  transfers between devices with their start and end apart: 3 -> 3, of which waited for: 3 -> 3; matrix products, arithmetic and copies ran while one was open for 16% -> 18% of each run, Pallas kernels for 0% -> 0%
where the time goes in v1:
time: 754 us; the launch traced here: 749 us
  waiting for transfers between devices  240 us (32%)
  local copies, waits for them, and re-layouts  235 us (31%)
  matrix products  123 us (16%)
  other arithmetic  97.6 us (13%)
  loops' own time  23.4 us (3%)
  starting transfers between devices  15.6 us (2%)
  between operations  14.4 us (2%)
    all_gather x1, waiting for transfers between devices, on_device(): key_piece = lax.all_gather(key_matrix_rows, 'seq', axis=0, tiled=True)  149 us
    gather x1, local copies, waits for them, and re-layouts, on_device(): slot_ids = page_slot[position // PAGE_TOKENS]  102 us
    all_to_all x1, waiting for transfers between devices, on_device(): tiles = lax.all_to_all(tiles, 'seq', split_axis=0, concat_axis=0)  69.1 us
    dot_general x16, matrix products, attend(): jnp.einsum('hgqk,khd->hgqd', weights.astype(jnp.bfloat16), value_heads, p...  53.3 us
    dynamic_slice x32, local copies, waits for them, and re-layouts, sub_step(): value_block = lax.dynamic_slice_in_dim(value_piece, offset, sub_width, 0)  49.2 us
    dot_general x16, matrix products, attend(): jnp.einsum('qhgd,khd->hgqk', queries, key_heads, preferred_element_type=j...  43.9 us
    reduce_sum x16, other arithmetic, attend(): new_sum = run_sum * factor + jnp.sum(weights, -1)  33.9 us
    another operation x1, loops' own time, on_device(): lax.scan(sub_step, absorb_state, jnp.arange(length // sub_width, dtype=jn...  23.1 us
  transfers between devices with their start and end apart: 3, of which 3 were waited for; matrix products, arithmetic and copies ran while one was open for 18% of the time, Pallas kernels for 0%

profile of v1, /device:TPU:1, one launch (start us, length us, event | category | flops | bytes accessed | tf_op | source)
XLA Modules:
  0.0 749.1 jit_solution(1787756860883533870)
XLA Ops:
  10.4 5.3 stack.5
  15.8 15.4 %all-to-all-start = ((bf16[128,128,256]{1,2,0:T(8,128)(2,1)}), bf16[128,128,256]{1,2,0:T(8,128)(2,1)}, u32[]{:S(2)}, u32[]{:S(2)}) async-start(bf16[128,128,256]{1,2,0:T(8,128)(2,1)} %stack.5), calls=%async_computation | async-start | bytes 16777216 | tf_op jit(solution)/shard_map/all_to_all | solution.py:143
  31.3 5.1 select_reduce_fusion
  36.9 101.9 %gather_fusion = s32[16384]{0:T(1024)S(1)} fusion(s32[512]{0:T(512)S(1)} %copy-done.1, s32[16384]{0:T(1024)S(1)} %broadcast_clamp_fusion), kind=kCustom, calls=%fused_computation | custom fusion | bytes 196608 | tf_op jit(solution)/shard_map/gather | solution.py:72
  150.1 69.1 %all-to-all-done = bf16[128,128,256]{1,2,0:T(8,128)(2,1)} async-done(((bf16[128,128,256]{1,2,0:T(8,128)(2,1)}), bf16[128,128,256]{1,2,0:T(8,128)(2,1)}, u32[]{:S(2)}, u32[]{:S(2)}) %all-to-all-start) | async-done | bytes 8388640 | tf_op jit(solution)/shard_map/all_to_all | solution.py:143
  219.2 12.0 %copy.73 = bf16[128,128,256]{2,1,0:T(8,128)(2,1)} copy(bf16[128,128,256]{1,2,0:T(8,128)(2,1)} %all-to-all-done) | data formatting | bytes 16777216 | tf_op jit(solution)/shard_map/all_to_all | solution.py:143
  231.2 149.2 %all-gather.2.cloned.1.call-done = bf16[16384,256]{1,0:T(8,128)(2,1)} async-done(((bf16[128,256]{1,0:T(8,128)(2,1)}), bf16[16384,256]{1,0:T(8,128)(2,1)}) %all-gather.2.cloned.1.call-update) | async-done | bytes 8388624 | tf_op jit(solution)/shard_map/all_gather | solution.py:140
  381.7 334.2 %while.19 = (s32[]{:T(128)}, f32[2,2,128]{2,1,0:T(2,128)S(1)}, f32[2,2,128]{2,1,0:T(2,128)S(1)}, f32[2,2,128,128]{3,2,1,0:T(8,128)}, f32[256,256]{1,0:T(8,128)S(...) while((s32[]{:T(128)}, f32[2,2,128]{2,1,0:T(2,128)S(1)}, ...), condition=%wide.region_11.12_spmd.clone, body=%wide.region_5.11_spmd.clone.sunk | while | flops 544936448 | bytes 16983412 | solution.py:170
  389.4 2.7 fusion.68
  392.2 2.1 fusion.70
  395.9 3.3 convolution_add_fusion.4
  409.0 2.7 fusion.68
  411.8 2.1 fusion.70
  415.5 3.3 convolution_add_fusion.4
  428.7 2.7 fusion.68
  431.5 2.1 fusion.70
  435.2 3.3 convolution_add_fusion.4
  448.4 2.7 fusion.68
  451.2 2.1 fusion.70
  454.9 3.3 convolution_add_fusion.4
  468.1 2.7 fusion.68
  470.8 2.1 fusion.70
  474.6 3.3 convolution_add_fusion.4
  480.0 2.4 conditional.3
  490.2 2.7 fusion.68
  492.9 2.1 fusion.70
  496.7 3.3 convolution_add_fusion.4
  502.1 2.4 conditional.3
  512.3 2.7 fusion.68
  515.0 2.1 fusion.70
  518.7 3.3 convolution_add_fusion.4
  532.0 2.7 fusion.68
  534.7 2.1 fusion.70
  538.4 3.3 convolution_add_fusion.4
  543.9 2.4 conditional.3
  554.1 2.7 fusion.68
  556.8 2.1 fusion.70
  560.5 3.3 convolution_add_fusion.4
  566.0 2.4 conditional.3
  576.2 2.7 fusion.68
  578.9 2.1 fusion.70
  582.6 3.3 convolution_add_fusion.4
  588.1 2.4 conditional.3
  598.3 2.7 fusion.68
  601.0 2.1 fusion.70
  604.7 3.3 convolution_add_fusion.4
  610.2 2.4 conditional.3
  620.4 2.7 fusion.68
  623.1 2.1 fusion.70
  626.8 3.3 convolution_add_fusion.4
  640.0 2.7 fusion.68
  642.8 2.1 fusion.70
  646.5 3.3 convolution_add_fusion.4
  659.7 2.7 fusion.68
  662.5 2.1 fusion.70
  666.2 3.3 convolution_add_fusion.4
  679.4 2.7 fusion.68
  682.2 2.1 fusion.70
  685.9 3.3 convolution_add_fusion.4
  691.3 2.4 conditional.3
  701.5 2.7 fusion.68
  708.0 3.3 convolution_add_fusion.4
  713.4 2.4 conditional.3
  719.1 21.5 %reduce-scatter.2.cloned.1.call-done = bf16[64,2048]{1,0:T(8,128)(2,1)} async-done(((bf16[128,2048]{1,0:T(8,128)(2,1)}), bf16[64,2048]{1,0:T(8,128)(2,1)}) %reduce-scatter.2.cloned.1.call-update) | async-done | bytes 262160 | tf_op jit(solution)/shard_map/reduce_scatter | solution.py:181
  (298 shorter events, 203.2 us)
Async XLA Ops:
  7.2 709.8 %copy-start = (bf16[512,2048]{1,0:T(8,128)(2,1)S(1)}, bf16[512,2048]{1,0:T(8,128)(2,1)}, u32[]{:S(2)}) copy-start(bf16[512,2048]{1,0:T(8,128)(2,1)} %param.18) | copy-start | bytes 6291460
  15.8 15.5 %copy-start.8 = (s32[128]{0:T(128)S(1)}, s32[128]{0:T(128)}, u32[]{:S(2)}) copy-start(s32[128]{0:T(128)} %param.20) | copy-start | bytes 1540
  15.8 203.5 %all-to-all-start = ((bf16[128,128,256]{1,2,0:T(8,128)(2,1)}), bf16[128,128,256]{1,2,0:T(8,128)(2,1)}, u32[]{:S(2)}, u32[]{:S(2)}) async-start(bf16[128,128,256]{1,2,0:T(8,128)(2,1)} %stack.5), calls=%async_computation | async-start | bytes 16777216 | tf_op jit(solution)/shard_map/all_to_all | solution.py:143
  31.1 5.7 copy-start.1
  31.2 349.2 %all-gather.2.cloned.1.call-start = ((), (), s32[]{:S(2)}) async-start(), calls=%async_computation.2 | async-start | bytes 8454144 | tf_op jit(solution)/shard_map/all_gather | solution.py:140
  36.9 102.7 %copy-start.9 = (s32[4]{0:T(128)S(1)}, s32[4]{0:T(128)}, u32[]{:S(2)}) copy-start(s32[4]{0:T(128)} %param.19) | copy-start | bytes 52
  36.9 102.9 %copy-start.4 = (bf16[128,2048]{1,0:T(8,128)(2,1)S(1)}, bf16[128,2048]{1,0:T(8,128)(2,1)}, u32[]{:S(2)}) copy-start(bf16[128,2048]{1,0:T(8,128)(2,1)} %param.13) | copy-start | bytes 1572868
  36.9 102.9 %copy-start.7 = (f32[2048]{0:T(1024)S(1)}, f32[2048]{0:T(1024)}, u32[]{:S(2)}) copy-start(f32[2048]{0:T(1024)} %param.14) | copy-start | bytes 24580
  142.7 88.5 %copy-start.6 = (s32[16384]{0:T(1024)}, s32[16384]{0:T(1024)S(1)}, u32[]{:S(2)}) copy-start(s32[16384]{0:T(1024)S(1)} %convert_reduce_fusion) | copy-start | bytes 196612
  145.7 594.9 %reduce-scatter.2.cloned.1.call-start = ((), (), s32[]{:S(2)}) async-start(), calls=%async_computation.3 | async-start | bytes 786432 | tf_op jit(solution)/shard_map/reduce_scatter | solution.py:181
  395.9 5.4 copy-start.2
  415.5 5.4 copy-start.2
  435.2 5.4 copy-start.2
  454.9 5.4 copy-start.2
  474.6 5.4 copy-start.2
  496.7 5.4 copy-start.2
  518.7 5.4 copy-start.2
  538.4 5.4 copy-start.2
  560.5 5.4 copy-start.2
  582.6 5.4 copy-start.2
  604.7 5.4 copy-start.2
  626.8 5.4 copy-start.2
  646.5 5.4 copy-start.2
  666.2 5.4 copy-start.2
  685.9 5.4 copy-start.2
  708.0 5.4 copy-start.2
  716.9 1.4 copy-start.3
  717.0 23.6 %copy-start.5 = (bf16[128,2048]{1,0:T(8,128)(2,1)S(1)}, bf16[128,2048]{1,0:T(8,128)(2,1)}, u32[]{:S(2)}) copy-start(bf16[128,2048]{1,0:T(8,128)(2,1)} %param.13) | copy-start | bytes 1572868
Sparse Core Ops, SparseCore 0:
  145.8 234.4 all-gather.1
  718.4 22.1 reduce-scatter.1
